TPU v7x, 256 devices: a whole 4x4x8 slice. The times are simulated.
256 devices in a mesh: row: 64 (over z, y, core), col: 4 (over x).
Axes of the slice: x: 4, y: 4, z: 8, core: 2. Of those that a mesh axis runs over, the one named last changes fastest.
Arguments:
- train_points: float32 [16, 3, 64, 128], P(None, None, 'row'), may hold values from -6 to 6
- new_points: float32 [16, 256], replicated, may hold values from -6 to 6
- lengthscales: float32 [16], replicated, may hold values from 2.5 to 6
- factor: float32 [3, 64, 128, 3, 4, 2048], P(None, 'row', None, None, 'col'), may hold values from -0.02734375 to 0.02734375
- diag_inverse: float32 [3, 64, 128, 4, 2048], P(None, 'row', None, 'col'), may hold values from -3 to 3
Outputs:
- solution: float32 [3, 4, 64, 32, 256], P(None, 'col', 'row')
All inputs are finite; a program needn't handle non-finite values.
Results may differ from a plain program's by a relative error of at most 0.0001.
Values sent between devices are 32-bit elements; how exact they have to be, the bound alone decides.
No kernel may reach another device: no remote copies, remote signals or barrier semaphores. Data moves between devices by JAX's collectives and lax.ppermute only.
A program may use at most 128 MiB of HBM per device.

v0:
```python
import jax
import jax.numpy as jnp
from jax import lax
from jax.sharding import PartitionSpec as P


def on_device(train_points, new_points, lengthscales, factor, diag_inverse):
    highest = lax.Precision.HIGHEST
    panels = factor.shape[0]
    block_rows = factor.shape[2]
    quarter_cols = factor.shape[5]
    new_count = new_points.shape[1]
    share_rows = block_rows // lax.axis_size("col")
    scaled_train = (train_points / lengthscales[:, None, None, None]).reshape(
        train_points.shape[0], panels * block_rows
    )
    scaled_new = new_points / lengthscales[:, None]
    inner_products = jnp.dot(scaled_train.T, scaled_new, precision=highest)
    sqdist = (
        jnp.sum(scaled_train * scaled_train, axis=0)[:, None]
        + jnp.sum(scaled_new * scaled_new, axis=0)[None, :]
        - 2.0 * inner_products
    )
    kernel = jnp.exp(-0.5 * sqdist).reshape(panels, block_rows, new_count)
    factor_blocks = factor.reshape(panels, block_rows, panels, quarter_cols)
    inverse_blocks = diag_inverse.reshape(panels, block_rows, quarter_cols)
    panel_numbers = jnp.arange(panels)

    def update(partial_rows, panel, quarter, after):
        column_slab = lax.dynamic_index_in_dim(factor_blocks, panel, axis=2, keepdims=False)
        change = jnp.einsum("piq,qm->pim", column_slab, quarter, precision=highest)
        below = (panel_numbers > after)[:, None, None]
        return partial_rows + jnp.where(below, change, 0.0)

    def advance(panel, loop_state):
        partial_rows, solved, pending = loop_state
        own_partial = lax.dynamic_index_in_dim(partial_rows, panel, 0, keepdims=False)
        summed = lax.psum(own_partial, "col")
        residual = lax.dynamic_index_in_dim(kernel, panel, 0, keepdims=False) - summed
        inverse_block = lax.dynamic_index_in_dim(inverse_blocks, panel, 0, keepdims=False)
        product = jnp.einsum("iq,im->qm", inverse_block, residual, precision=highest)
        own_rows = lax.psum_scatter(product, "row", scatter_dimension=0, tiled=True)
        quarter = lax.all_gather(own_rows, "row", axis=0, tiled=True)
        solved = lax.dynamic_update_index_in_dim(solved, own_rows, panel, 0)
        partial_rows = update(partial_rows, panel, quarter, panel)
        return (partial_rows, solved, pending)

    initial = (
        jnp.zeros((panels, block_rows, new_count), jnp.float32),
        jnp.zeros((panels, share_rows, new_count), jnp.float32),
        jnp.zeros((quarter_cols, new_count), jnp.float32),
    )
    partial_rows, solved, pending = lax.fori_loop(0, panels, advance, initial)
    return solved.reshape(panels, 1, 1, share_rows, new_count)


def solution(mesh):
    return jax.shard_map(
        on_device,
        mesh=mesh,
        in_specs=(
            P(None, None, "row", None),
            P(),
            P(),
            P(None, "row", None, None, "col", None),
            P(None, "row", None, "col", None),
        ),
        out_specs=P(None, "col", "row", None, None),
        check_vma=False,
    )
```

profile of v0, /device:TPU:1, one launch (start us, length us, event | category | flops | bytes accessed | tf_op | source)
XLA Modules:
  0.0 868.2 jit_solution(1024487664733539460)
XLA Ops:
  8.3 2.0 fusion.24
  10.3 12.1 %copy.15 = f32[3,1,128,3,1,2048]{5,2,0,3,4,1:T(8,128)} copy(f32[3,1,128,3,1,2048]{5,4,3,2,1,0:T(1,128)} %param.10) | data formatting | bytes 18874368 | tf_op args[3]
  22.4 1.4 copy.16
  23.8 837.8 %while.16 = (s32[]{:T(128)}, f32[3,128,256]{2,1,0:T(8,128)}, f32[3,32,256]{2,1,0:T(8,128)}, f32[3,128,3,2048]{3,1,0,2:T(8,128)}, f32[3,128,2048]{2,1,0:T(8,128)S...) while((s32[]{:T(128)}, f32[3,128,256]{2,1,0:T(8,128)}, f32[3,32,256]{2,1,0:T(8,128)}, ...), condition=%wide.region_5.6_spmd.clone, body=%wide.region_2.5_spmd.clone.sunk | while | flops 3221585920 | bytes 24118516 | solution.py:53
  24.9 50.3 %all-reduce.2.cloned.1.call-done = f32[128,256]{1,0:T(8,128)} async-done(((f32[128,256]{1,0:T(8,128)}), f32[128,256]{1,0:T(8,128)}) %all-reduce.2.cloned.1.call-update) | async-done | bytes 131088 | tf_op jit(solution)/shard_map/while/body/eval_jaxpr/psum | solution.py:38
  75.2 4.1 fusion.36
  79.4 138.6 %reduce-scatter.2.cloned.1.call-done = f32[32,256]{1,0:T(8,128)} async-done(((f32[2048,256]{1,0:T(8,128)}), f32[32,256]{1,0:T(8,128)}) %reduce-scatter.2.cloned.1.call-update) | async-done | bytes 32784 | tf_op jit(solution)/shard_map/while/body/eval_jaxpr/reduce_scatter | solution.py:42
  218.1 1.4 bitcast_dynamic-update-slice_fusion.2
  219.4 82.4 %all-gather.2.cloned.1.call-done = f32[2048,256]{1,0:T(8,128)} async-done(((f32[32,256]{1,0:T(8,128)}), f32[2048,256]{1,0:T(8,128)}) %all-gather.2.cloned.1.call-update) | async-done | bytes 2097168 | tf_op jit(solution)/shard_map/while/body/eval_jaxpr/all_gather | solution.py:43
  301.9 6.0 fusion.37
  307.8 1.0 broadcast_select_fusion.2
  309.6 42.5 %all-reduce.2.cloned.1.call-done = f32[128,256]{1,0:T(8,128)} async-done(((f32[128,256]{1,0:T(8,128)}), f32[128,256]{1,0:T(8,128)}) %all-reduce.2.cloned.1.call-update) | async-done | bytes 131088 | tf_op jit(solution)/shard_map/while/body/eval_jaxpr/psum | solution.py:38
  352.1 4.1 fusion.36
  356.3 138.2 %reduce-scatter.2.cloned.1.call-done = f32[32,256]{1,0:T(8,128)} async-done(((f32[2048,256]{1,0:T(8,128)}), f32[32,256]{1,0:T(8,128)}) %reduce-scatter.2.cloned.1.call-update) | async-done | bytes 32784 | tf_op jit(solution)/shard_map/while/body/eval_jaxpr/reduce_scatter | solution.py:42
  494.5 1.4 bitcast_dynamic-update-slice_fusion.2
  495.9 82.6 %all-gather.2.cloned.1.call-done = f32[2048,256]{1,0:T(8,128)} async-done(((f32[32,256]{1,0:T(8,128)}), f32[2048,256]{1,0:T(8,128)}) %all-gather.2.cloned.1.call-update) | async-done | bytes 2097168 | tf_op jit(solution)/shard_map/while/body/eval_jaxpr/all_gather | solution.py:43
  578.5 6.0 fusion.37
  584.5 1.0 broadcast_select_fusion.2
  586.2 42.8 %all-reduce.2.cloned.1.call-done = f32[128,256]{1,0:T(8,128)} async-done(((f32[128,256]{1,0:T(8,128)}), f32[128,256]{1,0:T(8,128)}) %all-reduce.2.cloned.1.call-update) | async-done | bytes 131088 | tf_op jit(solution)/shard_map/while/body/eval_jaxpr/psum | solution.py:38
  629.0 4.1 fusion.36
  633.2 138.6 %reduce-scatter.2.cloned.1.call-done = f32[32,256]{1,0:T(8,128)} async-done(((f32[2048,256]{1,0:T(8,128)}), f32[32,256]{1,0:T(8,128)}) %reduce-scatter.2.cloned.1.call-update) | async-done | bytes 32784 | tf_op jit(solution)/shard_map/while/body/eval_jaxpr/reduce_scatter | solution.py:42
  771.9 1.4 bitcast_dynamic-update-slice_fusion.2
  773.3 82.4 %all-gather.2.cloned.1.call-done = f32[2048,256]{1,0:T(8,128)} async-done(((f32[32,256]{1,0:T(8,128)}), f32[2048,256]{1,0:T(8,128)}) %all-gather.2.cloned.1.call-update) | async-done | bytes 2097168 | tf_op jit(solution)/shard_map/while/body/eval_jaxpr/all_gather | solution.py:43
  855.7 6.0 fusion.37
  (31 shorter events, 4.2 us)
Async XLA Ops:
  10.3 12.1 %copy-start = (f32[3,1,128,1,2048]{4,3,2,1,0:T(1,128)S(1)}, f32[3,1,128,1,2048]{4,3,2,1,0:T(1,128)}, u32[]{:S(2)}) copy-start(f32[3,1,128,1,2048]{4,3,2,1,0:T(1,128)} %param.11) | copy-start | bytes 9437188
  24.0 51.2 %all-reduce.2.cloned.1.call-start = ((), (), s32[]{:S(2)}) async-start(), calls=%async_computation.1 | async-start | bytes 262144 | tf_op jit(solution)/shard_map/while/body/eval_jaxpr/psum | solution.py:38
  24.8 193.2 %reduce-scatter.2.cloned.1.call-start = ((), (), s32[]{:S(2)}) async-start(), calls=%async_computation.2 | async-start | bytes 2129920 | tf_op jit(solution)/shard_map/while/body/eval_jaxpr/reduce_scatter | solution.py:42
  79.3 222.5 %all-gather.2.cloned.1.call-start = ((), (), s32[]{:S(2)}) async-start(), calls=%async_computation.3 | async-start | bytes 2129920 | tf_op jit(solution)/shard_map/while/body/eval_jaxpr/all_gather | solution.py:43
  307.8 44.3 %all-reduce.2.cloned.1.call-start = ((), (), s32[]{:S(2)}) async-start(), calls=%async_computation.1 | async-start | bytes 262144 | tf_op jit(solution)/shard_map/while/body/eval_jaxpr/psum | solution.py:38
  309.6 184.9 %reduce-scatter.2.cloned.1.call-start = ((), (), s32[]{:S(2)}) async-start(), calls=%async_computation.2 | async-start | bytes 2129920 | tf_op jit(solution)/shard_map/while/body/eval_jaxpr/reduce_scatter | solution.py:42
  356.2 222.2 %all-gather.2.cloned.1.call-start = ((), (), s32[]{:S(2)}) async-start(), calls=%async_computation.3 | async-start | bytes 2129920 | tf_op jit(solution)/shard_map/while/body/eval_jaxpr/all_gather | solution.py:43
  584.4 44.6 %all-reduce.2.cloned.1.call-start = ((), (), s32[]{:S(2)}) async-start(), calls=%async_computation.1 | async-start | bytes 262144 | tf_op jit(solution)/shard_map/while/body/eval_jaxpr/psum | solution.py:38
  586.2 185.7 %reduce-scatter.2.cloned.1.call-start = ((), (), s32[]{:S(2)}) async-start(), calls=%async_computation.2 | async-start | bytes 2129920 | tf_op jit(solution)/shard_map/while/body/eval_jaxpr/reduce_scatter | solution.py:42
  633.2 222.5 %all-gather.2.cloned.1.call-start = ((), (), s32[]{:S(2)}) async-start(), calls=%async_computation.3 | async-start | bytes 2129920 | tf_op jit(solution)/shard_map/while/body/eval_jaxpr/all_gather | solution.py:43
Sparse Core Ops, SparseCore 0:
  27.2 47.9 all-reduce.1
  79.8 138.1 reduce-scatter.1
  220.8 81.0 all-gather.1
  310.7 41.4 all-reduce.1
  356.6 137.9 reduce-scatter.1
  497.1 81.3 all-gather.1
  587.6 41.4 all-reduce.1
  633.6 138.1 reduce-scatter.1
  774.6 81.0 all-gather.1
where the time goes:
time: 869 us; the launch traced here: 868 us
  waiting for transfers between devices  799 us (92%)
  matrix products  32.3 us (4%)
  local copies, waits for them, and re-layouts  19.7 us (2%)
  between operations  13.1 us (2%)
    reduce_scatter x3, waiting for transfers between devices, advance(): own_rows = lax.psum_scatter(product, 'row', scatter_dimension=0, tiled=True)  415 us
    all_gather x3, waiting for transfers between devices, advance(): quarter = lax.all_gather(own_rows, 'row', axis=0, tiled=True)  247 us
    psum x3, waiting for transfers between devices, advance(): summed = lax.psum(own_partial, 'col')  136 us
    dot_general x3, matrix products, update(): change = jnp.einsum('piq,qm->pim', column_slab, quarter, precision=highest)  17.9 us
  transfers between devices with their start and end apart: 9, of which 9 were waited for; matrix products, arithmetic and copies ran while one was open for 0% of the time, Pallas kernels for 0%

commit v1 on v0

--- a/solution.py
+++ b/solution.py
@@ -35,7 +35,8 @@
     def advance(panel, loop_state):
         partial_rows, solved, pending = loop_state
         own_partial = lax.dynamic_index_in_dim(partial_rows, panel, 0, keepdims=False)
-        summed = lax.psum(own_partial, "col")
+        parts = lax.all_gather(own_partial, "col")
+        summed = jnp.sum(parts, axis=0)
         residual = lax.dynamic_index_in_dim(kernel, panel, 0, keepdims=False) - summed
         inverse_block = lax.dynamic_index_in_dim(inverse_blocks, panel, 0, keepdims=False)
         product = jnp.einsum("iq,im->qm", inverse_block, residual, precision=highest)

time: 869 us -> 759 us (0.87)
  waiting for transfers between devices: 799 us -> 659 us
  blocking collectives: 0 us -> 34.2 us
    psum x3 -> x0, waiting for transfers between devices: 136 us -> none  [advance(): summed = lax.psum(own_partial, 'col')]
    all_gather x0 -> x3, blocking collectives: none -> 34.2 us  [advance(): parts = lax.all_gather(own_partial, 'col')]
  transfers between devices with their start and end apart: 9 -> 6, of which waited for: 9 -> 6; matrix products, arithmetic and copies ran while one was open for 0% -> 1% of each run, Pallas kernels for 0% -> 0%
where the time goes in v1:
time: 759 us; the launch traced here: 758 us
  waiting for transfers between devices  659 us (87%)
  blocking collectives  34.2 us (5%)
  matrix products  30.1 us (4%)
  local copies, waits for them, and re-layouts  19.4 us (3%)
  between operations  13.4 us (2%)
    reduce_scatter x3, waiting for transfers between devices, advance(): own_rows = lax.psum_scatter(product, 'row', scatter_dimension=0, tiled=True)  410 us
    all_gather x3, waiting for transfers between devices, advance(): quarter = lax.all_gather(own_rows, 'row', axis=0, tiled=True)  249 us
    all_gather x3, blocking collectives, advance(): parts = lax.all_gather(own_partial, 'col')  34.2 us
    dot_general x3, matrix products, update(): change = jnp.einsum('piq,qm->pim', column_slab, quarter, precision=highest)  15.6 us
  transfers between devices with their start and end apart: 6, of which 6 were waited for; matrix products, arithmetic and copies ran while one was open for 1% of the time, Pallas kernels for 0%

profile of v1, /device:TPU:1, one launch (start us, length us, event | category | flops | bytes accessed | tf_op | source)
XLA Modules:
  0.0 758.5 jit_solution(3933065390499230057)
XLA Ops:
  6.5 0.9 fusion.28
  7.4 0.8 multiply_reduce_fusion.1
  8.3 1.3 fusion.25
  9.6 12.1 %copy.16 = f32[3,1,128,3,1,2048]{5,2,0,3,4,1:T(8,128)} copy(f32[3,1,128,3,1,2048]{5,4,3,2,1,0:T(1,128)} %param.10) | data formatting | bytes 18874368 | tf_op args[3]
  21.7 3.0 copy.17
  24.7 726.9 %while.16 = (s32[]{:T(128)}, f32[3,128,256]{2,1,0:T(8,128)S(1)}, f32[3,32,256]{2,1,0:T(8,128)}, f32[3,128,3,2048]{3,1,0,2:T(8,128)}, f32[3,128,2048]{2,1,0:T(8,1...) while((s32[]{:T(128)}, f32[3,128,256]{2,1,0:T(8,128)S(1)}, ...), condition=%wide.region_5.6_spmd.clone, body=%wide.region_2.5_spmd.clone.sunk | while | flops 3221651456 | bytes 24642776 | solution.py:54
  24.8 12.3 %all_gather.19 = f32[4,128,256]{2,1,0:T(8,128)S(1)} all-gather(f32[1,128,256]{2,1,0:T(8,128)S(1)} %constant_dynamic-slice_fusion.2), channel_id=1, replica_groups=mesh['row'=64,'col'=4] {'col'}, dimensions={0}, use_global_device_ids=true | all-gather | bytes 655360 | tf_op jit(solution)/shard_map/while/body/eval_jaxpr/all_gather | solution.py:38
  37.1 4.4 fusion.39
  41.6 140.4 %reduce-scatter.2.cloned.1.call-done = f32[32,256]{1,0:T(8,128)} async-done(((f32[2048,256]{1,0:T(8,128)}), f32[32,256]{1,0:T(8,128)}) %reduce-scatter.2.cloned.1.call-update) | async-done | bytes 32784 | tf_op jit(solution)/shard_map/while/body/eval_jaxpr/reduce_scatter | solution.py:43
  182.0 1.4 bitcast_dynamic-update-slice_fusion.2
  183.4 82.8 %all-gather.2.cloned.1.call-done = f32[2048,256]{1,0:T(8,128)} async-done(((f32[32,256]{1,0:T(8,128)}), f32[2048,256]{1,0:T(8,128)}) %all-gather.2.cloned.1.call-update) | async-done | bytes 2097168 | tf_op jit(solution)/shard_map/while/body/eval_jaxpr/all_gather | solution.py:44
  266.3 5.2 fusion.40
  271.6 10.9 %all_gather.19 = f32[4,128,256]{2,1,0:T(8,128)S(1)} all-gather(f32[1,128,256]{2,1,0:T(8,128)S(1)} %constant_dynamic-slice_fusion.2), channel_id=1, replica_groups=mesh['row'=64,'col'=4] {'col'}, dimensions={0}, use_global_device_ids=true | all-gather | bytes 655360 | tf_op jit(solution)/shard_map/while/body/eval_jaxpr/all_gather | solution.py:38
  282.6 4.4 fusion.39
  287.1 135.1 %reduce-scatter.2.cloned.1.call-done = f32[32,256]{1,0:T(8,128)} async-done(((f32[2048,256]{1,0:T(8,128)}), f32[32,256]{1,0:T(8,128)}) %reduce-scatter.2.cloned.1.call-update) | async-done | bytes 32784 | tf_op jit(solution)/shard_map/while/body/eval_jaxpr/reduce_scatter | solution.py:43
  422.2 1.4 bitcast_dynamic-update-slice_fusion.2
  423.6 82.8 %all-gather.2.cloned.1.call-done = f32[2048,256]{1,0:T(8,128)} async-done(((f32[32,256]{1,0:T(8,128)}), f32[2048,256]{1,0:T(8,128)}) %all-gather.2.cloned.1.call-update) | async-done | bytes 2097168 | tf_op jit(solution)/shard_map/while/body/eval_jaxpr/all_gather | solution.py:44
  506.3 5.2 fusion.40
  511.7 10.9 %all_gather.19 = f32[4,128,256]{2,1,0:T(8,128)S(1)} all-gather(f32[1,128,256]{2,1,0:T(8,128)S(1)} %constant_dynamic-slice_fusion.2), channel_id=1, replica_groups=mesh['row'=64,'col'=4] {'col'}, dimensions={0}, use_global_device_ids=true | all-gather | bytes 655360 | tf_op jit(solution)/shard_map/while/body/eval_jaxpr/all_gather | solution.py:38
  522.7 4.4 fusion.39
  527.2 134.7 %reduce-scatter.2.cloned.1.call-done = f32[32,256]{1,0:T(8,128)} async-done(((f32[2048,256]{1,0:T(8,128)}), f32[32,256]{1,0:T(8,128)}) %reduce-scatter.2.cloned.1.call-update) | async-done | bytes 32784 | tf_op jit(solution)/shard_map/while/body/eval_jaxpr/reduce_scatter | solution.py:43
  662.0 1.4 bitcast_dynamic-update-slice_fusion.2
  663.3 83.1 %all-gather.2.cloned.1.call-done = f32[2048,256]{1,0:T(8,128)} async-done(((f32[32,256]{1,0:T(8,128)}), f32[2048,256]{1,0:T(8,128)}) %all-gather.2.cloned.1.call-update) | async-done | bytes 2097168 | tf_op jit(solution)/shard_map/while/body/eval_jaxpr/all_gather | solution.py:44
  746.4 5.2 fusion.40
  (28 shorter events, 0.6 us)
Async XLA Ops:
  9.5 12.1 %copy-start = (f32[3,1,128,1,2048]{4,3,2,1,0:T(1,128)S(1)}, f32[3,1,128,1,2048]{4,3,2,1,0:T(1,128)}, u32[]{:S(2)}) copy-start(f32[3,1,128,1,2048]{4,3,2,1,0:T(1,128)} %param.11) | copy-start | bytes 9437188
  24.7 157.3 %reduce-scatter.2.cloned.1.call-start = ((), (), s32[]{:S(2)}) async-start(), calls=%async_computation.1 | async-start | bytes 2129920 | tf_op jit(solution)/shard_map/while/body/eval_jaxpr/reduce_scatter | solution.py:43
  41.6 224.7 %all-gather.2.cloned.1.call-start = ((), (), s32[]{:S(2)}) async-start(), calls=%async_computation.2 | async-start | bytes 2129920 | tf_op jit(solution)/shard_map/while/body/eval_jaxpr/all_gather | solution.py:44
  271.5 150.7 %reduce-scatter.2.cloned.1.call-start = ((), (), s32[]{:S(2)}) async-start(), calls=%async_computation.1 | async-start | bytes 2129920 | tf_op jit(solution)/shard_map/while/body/eval_jaxpr/reduce_scatter | solution.py:43
  287.0 219.3 %all-gather.2.cloned.1.call-start = ((), (), s32[]{:S(2)}) async-start(), calls=%async_computation.2 | async-start | bytes 2129920 | tf_op jit(solution)/shard_map/while/body/eval_jaxpr/all_gather | solution.py:44
  511.6 150.3 %reduce-scatter.2.cloned.1.call-start = ((), (), s32[]{:S(2)}) async-start(), calls=%async_computation.1 | async-start | bytes 2129920 | tf_op jit(solution)/shard_map/while/body/eval_jaxpr/reduce_scatter | solution.py:43
  527.1 219.3 %all-gather.2.cloned.1.call-start = ((), (), s32[]{:S(2)}) async-start(), calls=%async_computation.2 | async-start | bytes 2129920 | tf_op jit(solution)/shard_map/while/body/eval_jaxpr/all_gather | solution.py:44
Sparse Core Ops, SparseCore 0:
  41.7 140.2 reduce-scatter.1
  185.2 81.0 all-gather.1
  287.2 134.9 reduce-scatter.1
  425.2 81.1 all-gather.1
  527.2 134.6 reduce-scatter.1
  664.9 81.4 all-gather.1
